TPU v7x, 128 devices: a whole 4x4x4 slice. The times are simulated.
128 devices in a mesh: mode: 32 (over x, y, core), wall: 2 (over z_lo), ckpt: 2 (over z_hi).
Axes of the slice: x: 4, y: 4, z: 4 (z_hi: 2, z_lo: 2; z = z_hi * 2 + z_lo), core: 2. Of those that a mesh axis runs over, the one named last changes fastest.
Arguments:
- adjoint: float32 [2, 5, 1024, 4096], P(None, None, ('wall', 'ckpt'), 'mode'), may hold values from -6 to 6
- forward: float32 [2, 2, 1024, 4096], P('ckpt', None, 'wall', 'mode'), may hold values from -0.09375 to 0.09375
- mode_map: int32 [4096], P('mode'), may hold values from 0 to 4095, as said below
Outputs:
- adjoint_prev: float32 [2, 5, 1024, 4096], P(None, None, ('wall', 'ckpt'), 'mode')
Inputs may be any that keep to these rules, and one draw needn't show every extreme that they name: mode_map is a permutation of the 64 x 64 modes laid out by frequency: for every block b of 64 consecutive slots there is a frequency p(b) such that slot b * 64 + r holds mode p(b) * 64 + r, and p takes every frequency once.
All inputs are finite; a program needn't handle non-finite values.
Results may differ from a plain program's by a relative error of at most 0.0001.
Values sent between devices are 32-bit elements; how exact they have to be, the bound alone decides.
A program may use at most 128 MiB of HBM per device.

v0:
```python
import math
import jax
import jax.numpy as jnp
from jax import lax
from jax.sharding import PartitionSpec as P

NF = 64
NK = 64
MODES = 4096
KAPPA = 0.2
COUPLING = 0.5
HIGHEST = lax.Precision.HIGHEST


def with_halo(block, sides, width):
    for axis, dim in sides:
        count = lax.axis_size(axis)
        forward = [(i, i + 1) for i in range(count - 1)]
        backward = [(target, source) for source, target in forward]
        low = lax.ppermute(
            lax.slice_in_dim(block, block.shape[dim] - width, None, axis=dim), axis, forward
        )
        high = lax.ppermute(lax.slice_in_dim(block, 0, width, axis=dim), axis, backward)
        block = jnp.concatenate([low, block, high], axis=dim)
    return block


def entering(value, axis, join, neutral):
    count, mine = (lax.axis_size(axis), lax.axis_index(axis))
    pieces = lax.all_gather(value, axis)
    so_far = jnp.full_like(value, 0) + jnp.asarray(neutral, value.dtype)

    def turn(position, so_far):
        longer = join(so_far, pieces[position])
        return jnp.where(position < mine, longer, so_far)

    return lax.fori_loop(0, count - 1, turn, so_far)


def add_pair(earlier, later):
    return earlier + later


def rates(grid_index):
    freq_index = grid_index // NK
    span_index = grid_index % NK
    freq_signed = (freq_index + NF // 2) % NF - NF // 2
    span_signed = (span_index + NK // 2) % NK - NK // 2
    return (2.0 / NF * freq_signed.astype(jnp.float32), 2.0 / NK * span_signed.astype(jnp.float32))


def span_tables(direction):
    col_ids = jnp.arange(NK, dtype=jnp.int32)
    phase_cols = 2.0 * math.pi / NK * (col_ids[:, None] * col_ids[None, :] % NK).astype(jnp.float32)
    return (jnp.cos(phase_cols), direction * jnp.sin(phase_cols))


def row_tables(direction, out_ids, in_ids):
    phase_rows = 2.0 * math.pi / NF * (out_ids[:, None] * in_ids[None, :] % NF).astype(jnp.float32)
    return (jnp.cos(phase_rows), direction * jnp.sin(phase_rows))


def span_dft(real_part, imag_part, direction):
    cosine, sine_part = span_tables(direction)
    real_cos = jnp.einsum("...k,kz->...z", real_part, cosine, precision=HIGHEST)
    real_sin = jnp.einsum("...k,kz->...z", real_part, sine_part, precision=HIGHEST)
    imag_cos = jnp.einsum("...k,kz->...z", imag_part, cosine, precision=HIGHEST)
    imag_sin = jnp.einsum("...k,kz->...z", imag_part, sine_part, precision=HIGHEST)
    return (real_cos - imag_sin, real_sin + imag_cos)


def lead_dft(real_part, imag_part, direction, out_ids, in_ids):
    cos_rows, sin_rows = row_tables(direction, out_ids, in_ids)
    lead_shape = real_part.shape
    flat_real = real_part.reshape(lead_shape[0], -1)
    flat_imag = imag_part.reshape(lead_shape[0], -1)
    out_real = jnp.dot(cos_rows, flat_real, precision=HIGHEST) - jnp.dot(
        sin_rows, flat_imag, precision=HIGHEST
    )
    out_imag = jnp.dot(sin_rows, flat_real, precision=HIGHEST) + jnp.dot(
        cos_rows, flat_imag, precision=HIGHEST
    )
    return (out_real.reshape(lead_shape), out_imag.reshape(lead_shape))


def to_physical(real_part, imag_part, out_ids, in_ids):
    shape_front = real_part.shape[:-1] + (NF, NK)
    span_real, span_imag = span_dft(
        real_part.reshape(shape_front), imag_part.reshape(shape_front), 1.0
    )
    span_real = jnp.moveaxis(span_real, -2, 0)
    span_imag = jnp.moveaxis(span_imag, -2, 0)
    return lead_dft(span_real, span_imag, 1.0, out_ids, in_ids)


def to_spectral(real_part, imag_part, out_ids, in_ids):
    lead_real, lead_imag = lead_dft(real_part, imag_part, -1.0, out_ids, in_ids)
    lead_real = jnp.moveaxis(lead_real, 0, -2)
    lead_imag = jnp.moveaxis(lead_imag, 0, -2)
    span_real, span_imag = span_dft(lead_real, lead_imag, -1.0)
    shape_front = span_real.shape[:-2] + (MODES,)
    return (span_real.reshape(shape_front), span_imag.reshape(shape_front))


def coupling_term(adjoint_slots, forward_phys, block_freq, time_ids):
    a_real, a_imag = to_physical(adjoint_slots[0], adjoint_slots[1], time_ids, block_freq)
    w_real = forward_phys[0][:, None]
    w_imag = forward_phys[1][:, None]
    prod_real = w_real * a_real + w_imag * a_imag
    prod_imag = w_real * a_imag - w_imag * a_real
    real_part, imag_part = to_spectral(prod_real, prod_imag, block_freq, time_ids)
    return jnp.stack([real_part, imag_part]) / (NF * NK)


def add_continuity(stepped, running, row_scale):
    updated_v = jnp.stack(
        [stepped[0, 1] + running[1] * row_scale, stepped[1, 1] - running[0] * row_scale]
    )
    return jnp.concatenate([stepped[:, :1], updated_v[:, None], stepped[:, 2:]], 1)


def wall_step_modes(current, coupled, alpha_rate, beta_rate, row_scale):
    padded = with_halo(current, ((("wall", "ckpt"), 2),), 1)
    stepped = (
        current
        + KAPPA * (padded[:, :, 2:] - 2.0 * current + padded[:, :, :-2])
        - COUPLING * coupled
    )
    source = alpha_rate * stepped[:, 0] + beta_rate * stepped[:, 2]
    row_count = current.shape[2]
    row_ids = jnp.arange(row_count, dtype=jnp.int32)
    lower_ones = (row_ids[:, None] >= row_ids[None, :]).astype(jnp.float32)
    running = jnp.einsum("yv,cvm->cym", lower_ones, source, precision=HIGHEST)
    totals = running[:, -1]
    before = entering(totals, ("wall", "ckpt"), add_pair, jnp.zeros_like(totals))
    running = running + before[:, None]
    return add_continuity(stepped, running, row_scale)


def to_modes(values):
    return lax.all_to_all(values, "mode", split_axis=3, concat_axis=2, tiled=True)


def on_device(adjoint, forward, mode_map):
    station_count = lax.axis_size("ckpt")
    row_scale = 1.0 / math.sqrt(adjoint.shape[2] * lax.axis_size("wall") * lax.axis_size("ckpt"))
    stored = lax.all_gather(forward, "ckpt", axis=0, tiled=True)
    row_count = adjoint.shape[2]
    own_rows = lax.dynamic_slice_in_dim(stored, lax.axis_index("ckpt") * row_count, row_count, 2)
    full_map = lax.all_gather(mode_map, "mode", axis=0, tiled=True)
    block_freq = full_map.reshape(NF, NK)[:, 0] // NK
    time_ids = jnp.arange(NF, dtype=jnp.int32)
    adjoint_cols, forward_cols = (
        lax.all_to_all(adjoint, "mode", split_axis=2, concat_axis=3, tiled=True),
        lax.all_to_all(own_rows, "mode", split_axis=2, concat_axis=3, tiled=True),
    )
    phys_real, phys_imag = to_physical(forward_cols[:, 0], forward_cols[:, 1], time_ids, block_freq)
    local_alpha, local_beta = rates(mode_map)
    current = adjoint
    for station in range(station_count - 1, -1, -1):
        if station == station_count - 1:
            columns = adjoint_cols
        else:
            columns = lax.all_to_all(current, "mode", split_axis=2, concat_axis=3, tiled=True)
        station_phys = (phys_real[:, station], phys_imag[:, station])
        coupled = to_modes(coupling_term(columns, station_phys, block_freq, time_ids))
        current = wall_step_modes(current, coupled, local_alpha, local_beta, row_scale)
    return current


def solution(mesh):
    placed = (P(None, None, ("wall", "ckpt"), "mode"), P("ckpt", None, "wall", "mode"), P("mode"))
    return jax.shard_map(
        on_device,
        mesh=mesh,
        in_specs=placed,
        out_specs=P(None, None, ("wall", "ckpt"), "mode"),
        check_vma=False,
    )
```

profile of v0, /device:TPU:0, one launch (start us, length us, event | category | flops | bytes accessed | tf_op | source)
XLA Modules:
  0.0 545.5 jit_solution(10773207464401871965)
XLA Ops:
  6.5 3.5 copy.215
  10.0 7.6 %all-to-all-start.1 = ((f32[2,5,256,128]{3,1,0,2:T(8,128)}), f32[2,5,256,128]{3,1,0,2:T(8,128)S(1)}, u32[]{:S(2)}, u32[]{:S(2)}) async-start(f32[2,5,256,128]{3,1,0,2:T(8,128)} %copy.215), calls=%async_computation.1 | async-start | bytes 4194304 | tf_op jit(solution)/shard_map/all_to_all | solution.py:154
  18.3 40.0 %all-gather.2 = s32[32,1,128]{2,1,0:T(1,128)S(1)} all-gather(s32[1,1,128]{2,1,0:T(1,128)S(1)} %bitcast.305), channel_id=1, replica_groups=mesh['mode'=32,'wall'=2,'ckpt'=2] {'mode'}, dimensions={0}, use_global_device_ids=true | all-gather | bytes 16896 | tf_op jit(solution)/shard_map/all_gather | solution.py:150
  62.0 5.8 %all-to-all-start = ((f32[2,2,256,128]{3,1,0,2:T(2,128)}), f32[2,2,256,128]{3,1,0,2:T(2,128)}, u32[]{:S(2)}, u32[]{:S(2)}) async-start(f32[2,2,256,128]{3,1,0,2:T(2,128)} %copy.211), calls=%async_computation | async-start | bytes 1048576 | tf_op jit(solution)/shard_map/all_to_all | solution.py:155
  68.9 5.1 fusion.64
  74.0 5.1 fusion.76
  80.5 4.0 convolution_subtract_fusion.7
  84.5 4.0 convolution_add_fusion.7
  92.4 2.5 convolution_add_fusion.3
  113.1 3.2 multiply_subtract_fusion.1
  120.4 2.4 fusion.21
  127.3 3.7 convolution_subtract_fusion.6
  132.7 2.4 convolution_add_fusion.6
  137.0 17.9 %copy.223 = f32[2,5,8,4096]{2,0,1,3:T(2,128)} copy(f32[2,5,8,4096]{3,2,1,0:T(8,128)S(1)} %maximum_multiply_fusion) | data formatting | bytes 2621440 | tf_op jit(solution)/shard_map/div | solution.py:112
  154.8 31.2 %reshape.142 = f32[32,1,10240]{2,1,0:T(1,128)} reshape(f32[4096,5,2,8]{3,2,1,0:T(2,128)} %bitcast.284) | data formatting | bytes 2621440
  186.0 7.6 %all-to-all-start.2 = ((f32[32,1,10240]{2,1,0:T(1,128)}), f32[32,1,10240]{2,1,0:T(1,128)}, u32[]{:S(2)}, u32[]{:S(2)}) async-start(f32[32,1,10240]{2,1,0:T(1,128)} %reshape.142), calls=%async_computation.2 | async-start | bytes 2621440 | tf_op jit(solution)/shard_map/all_to_all | solution.py:141
  194.9 6.4 %collective-permute-start.1 = (f32[2,5,1,128]{3,0,2,1:T(2,128)S(1)}, f32[2,5,1,128]{3,0,2,1:T(2,128)S(1)}, u32[]{:S(2)}, u32[]{:S(2)}) collective-permute-start(f32[2,5,1,128]{3,0,2,1:T(2,128)S(1)} %copy.261), channel_id=1, source_target_pairs={{0,1},{1,2},{2,3},{4,5},{5,6},{6,7},{8,9},{9,10},{10,11},{12,13},{... | collective-permute-start | bytes 15368 | tf_op jit(solution)/shard_map/ppermute | solution.py:20
  203.8 9.6 %all-to-all-done.2 = f32[32,1,10240]{2,1,0:T(1,128)} async-done(((f32[32,1,10240]{2,1,0:T(1,128)}), f32[32,1,10240]{2,1,0:T(1,128)}, u32[]{:S(2)}, u32[]{:S(2)}) %all-to-all-start.2) | async-done | bytes 1310752 | tf_op jit(solution)/shard_map/all_to_all | solution.py:141
  213.9 5.1 reduce.4
  219.0 41.4 %reshape.143 = f32[4096,5,2,8]{3,2,1,0:T(2,128)} reshape(f32[32,10240]{1,0:T(8,128)S(1)} %reduce.4) | data formatting | bytes 2621440
  260.4 21.6 %copy.224 = f32[2,5,8,4096]{3,2,1,0:T(8,128)S(1)} copy(f32[2,5,8,4096]{2,0,1,3:T(2,128)} %bitcast.285) | data formatting | bytes 2621440 | tf_op jit(solution)/shard_map/all_to_all | solution.py:141
  284.6 2.4 fusion.9
  287.6 11.3 %all-gather = f32[8,1,128]{2,1,0:T(1,128)S(1)} all-gather(f32[2,1,128]{2,1,0:T(1,128)S(1)} %copy.227), channel_id=2, replica_groups=mesh['mode'=32,'wall'=2,'ckpt'=2] {'wall','ckpt'}, dimensions={0}, use_global_device_ids=true | all-gather | bytes 5120 | tf_op jit(solution)/shard_map/all_gather | solution.py:30
  302.0 4.1 all-to-all-start.3
  308.3 2.5 mul.490
  312.8 2.5 mul.494
  315.3 10.4 %all-to-all-done.3 = f32[2,5,256,128]{3,0,1,2:T(2,128)S(1)} async-done(((f32[2,5,256,128]{3,0,1,2:T(2,128)}), f32[2,5,256,128]{3,0,1,2:T(2,128)S(1)}, u32[]{:S(2)}, u32[]{:S(2)}) %all-to-all-start.3) | async-done | bytes 1310752 | tf_op jit(solution)/shard_map/all_to_all | solution.py:164
  329.1 2.4 fusion.79
  331.5 2.4 fusion.69
  336.1 2.6 fusion
  340.6 2.5 reshape.116
  343.0 2.9 fusion.141
  362.6 2.4 fusion.15
  365.0 2.4 fusion.13
  370.5 3.7 convolution_subtract_fusion.4
  374.3 2.6 stack_reshape.14
  376.9 3.7 convolution_add_fusion.4
  380.6 2.6 stack_reshape.15
  384.5 17.9 %copy.240 = f32[2,5,8,4096]{2,0,1,3:T(2,128)} copy(f32[2,5,8,4096]{3,2,1,0:T(8,128)S(1)} %maximum_multiply_fusion.1) | data formatting | bytes 2621440 | tf_op jit(solution)/shard_map/div | solution.py:112
  402.4 31.4 %reshape.144 = f32[32,1,10240]{2,1,0:T(1,128)} reshape(f32[4096,5,2,8]{3,2,1,0:T(2,128)} %bitcast.286) | data formatting | bytes 2621440
  433.8 4.0 all-to-all-start.4
  442.9 6.1 %collective-permute-start.3 = (f32[2,5,1,128]{3,0,2,1:T(2,128)S(1)}, f32[2,5,1,128]{3,0,2,1:T(2,128)S(1)}, u32[]{:S(2)}, u32[]{:S(2)}) collective-permute-start(f32[2,5,1,128]{3,0,2,1:T(2,128)S(1)} %copy.230), channel_id=1, source_target_pairs={{0,1},{1,2},{2,3},{4,5},{5,6},{6,7},{8,9},{9,10},{10,11},{12,13},{... | collective-permute-start | bytes 15368 | tf_op jit(solution)/shard_map/ppermute | solution.py:20
  451.4 6.1 %all-to-all-done.4 = f32[32,1,10240]{2,1,0:T(1,128)S(1)} async-done(((f32[32,1,10240]{2,1,0:T(1,128)}), f32[32,1,10240]{2,1,0:T(1,128)S(1)}, u32[]{:S(2)}, u32[]{:S(2)}) %all-to-all-start.4) | async-done | bytes 1310752 | tf_op jit(solution)/shard_map/all_to_all | solution.py:141
  457.5 3.7 reduce.5
  461.2 41.1 %reshape.145 = f32[4096,5,2,8]{3,2,1,0:T(2,128)} reshape(f32[32,10240]{1,0:T(8,128)S(1)} %reduce.5) | data formatting | bytes 2621440
  502.4 21.6 %copy.241 = f32[2,5,8,4096]{3,2,1,0:T(8,128)S(1)} copy(f32[2,5,8,4096]{2,0,1,3:T(2,128)} %bitcast.287) | data formatting | bytes 2621440 | tf_op jit(solution)/shard_map/all_to_all | solution.py:141
  525.5 2.7 copy_subtract_fusion
  528.9 7.8 %all-gather.1 = f32[8,1,128]{2,1,0:T(1,128)S(1)} all-gather(f32[2,1,128]{2,1,0:T(1,128)S(1)} %copy.246), channel_id=3, replica_groups=mesh['mode'=32,'wall'=2,'ckpt'=2] {'wall','ckpt'}, dimensions={0}, use_global_device_ids=true | all-gather | bytes 5120 | tf_op jit(solution)/shard_map/all_gather | solution.py:30
  (170 shorter events, 95.8 us)
Async XLA Ops:
  10.0 8.3 %copy-start.18 = (s32[128]{0:T(128)S(1)}, s32[128]{0:T(128)}, u32[]{:S(2)}) copy-start(s32[128]{0:T(128)} %param.9) | copy-start | bytes 1540
  10.0 52.0 %all-to-all-start.1 = ((f32[2,5,256,128]{3,1,0,2:T(8,128)}), f32[2,5,256,128]{3,1,0,2:T(8,128)S(1)}, u32[]{:S(2)}, u32[]{:S(2)}) async-start(f32[2,5,256,128]{3,1,0,2:T(8,128)} %copy.215), calls=%async_computation.1 | async-start | bytes 4194304 | tf_op jit(solution)/shard_map/all_to_all | solution.py:154
  17.6 42.1 %all-gather.5.cloned.1.call-start = ((), (), s32[]{:S(2)}) async-start(), calls=%async_computation.5 | async-start | bytes 1572864 | tf_op jit(solution)/shard_map/all_gather | solution.py:147
  62.0 32.9 %all-to-all-start = ((f32[2,2,256,128]{3,1,0,2:T(2,128)}), f32[2,2,256,128]{3,1,0,2:T(2,128)}, u32[]{:S(2)}, u32[]{:S(2)}) async-start(f32[2,2,256,128]{3,1,0,2:T(2,128)} %copy.211), calls=%async_computation | async-start | bytes 1048576 | tf_op jit(solution)/shard_map/all_to_all | solution.py:155
  79.1 1.3 copy-start.7
  80.5 4.0 copy-start.6
  105.8 1.0 copy-start.17
  122.8 1.3 copy-start.13
  186.0 7.6 %copy-start.4 = (f32[2,5,256,128]{3,2,1,0:T(8,128)S(1)}, f32[2,5,256,128]{3,2,1,0:T(8,128)}, u32[]{:S(2)}) copy-start(f32[2,5,256,128]{3,2,1,0:T(8,128)} %param.7) | copy-start | bytes 3932164
  186.0 27.3 %all-to-all-start.2 = ((f32[32,1,10240]{2,1,0:T(1,128)}), f32[32,1,10240]{2,1,0:T(1,128)}, u32[]{:S(2)}, u32[]{:S(2)}) async-start(f32[32,1,10240]{2,1,0:T(1,128)} %reshape.142), calls=%async_computation.2 | async-start | bytes 2621440 | tf_op jit(solution)/shard_map/all_to_all | solution.py:141
  193.6 8.2 %collective-permute-start = (f32[2,5,1,128]{3,0,2,1:T(2,128)S(1)}, f32[2,5,1,128]{3,0,2,1:T(2,128)S(1)}, u32[]{:S(2)}, u32[]{:S(2)}) collective-permute-start(f32[2,5,1,128]{3,0,2,1:T(2,128)S(1)} %copy.260), channel_id=1, source_target_pairs={{1,0},{2,1},{3,2},{5,4},{6,5},{7,6},{9,8},{10,9},{11,10},{13,12},{... | collective-permute-start | bytes 15368 | tf_op jit(solution)/shard_map/ppermute | solution.py:23
  194.9 7.7 %collective-permute-start.1 = (f32[2,5,1,128]{3,0,2,1:T(2,128)S(1)}, f32[2,5,1,128]{3,0,2,1:T(2,128)S(1)}, u32[]{:S(2)}, u32[]{:S(2)}) collective-permute-start(f32[2,5,1,128]{3,0,2,1:T(2,128)S(1)} %copy.261), channel_id=1, source_target_pairs={{0,1},{1,2},{2,3},{4,5},{5,6},{6,7},{8,9},{9,10},{10,11},{12,13},{... | collective-permute-start | bytes 15368 | tf_op jit(solution)/shard_map/ppermute | solution.py:20
  287.1 12.1 %copy-start.15 = (f32[2,1,256,128]{2,3,0,1:T(8,128)}, f32[2,1,256,128]{2,3,0,1:T(8,128)S(1)}, u32[]{:S(2)}) copy-start(f32[2,1,256,128]{2,3,0,1:T(8,128)S(1)} %slice.157) | copy-start | bytes 786436
  299.2 0.7 copy-start.16
  302.0 23.7 %all-to-all-start.3 = ((f32[2,5,256,128]{3,0,1,2:T(2,128)}), f32[2,5,256,128]{3,0,1,2:T(2,128)S(1)}, u32[]{:S(2)}, u32[]{:S(2)}) async-start(f32[2,5,256,128]{3,0,1,2:T(2,128)} %copy.232), calls=%async_computation.3 | async-start | bytes 2621440 | tf_op jit(solution)/shard_map/all_to_all | solution.py:164
  331.5 2.4 copy-start.9
  343.0 2.9 copy-start.3
  343.0 4.5 copy-start.5
  350.7 2.6 copy-start.14
  352.4 0.8 copy-start.2
  353.2 1.1 copy-start.8
  353.2 1.3 copy-start.10
  353.3 1.5 copy-start.11
  356.8 2.7 copy-start
  365.0 2.4 copy-start.1
  365.0 2.4 copy-start.12
  433.8 23.7 %all-to-all-start.4 = ((f32[32,1,10240]{2,1,0:T(1,128)}), f32[32,1,10240]{2,1,0:T(1,128)S(1)}, u32[]{:S(2)}, u32[]{:S(2)}) async-start(f32[32,1,10240]{2,1,0:T(1,128)} %reshape.144), calls=%async_computation.4 | async-start | bytes 2621440 | tf_op jit(solution)/shard_map/all_to_all | solution.py:141
  440.3 8.7 %collective-permute-start.2 = (f32[2,5,1,128]{3,0,2,1:T(2,128)S(1)}, f32[2,5,1,128]{3,0,2,1:T(2,128)S(1)}, u32[]{:S(2)}, u32[]{:S(2)}) collective-permute-start(f32[2,5,1,128]{3,0,2,1:T(2,128)S(1)} %copy.228), channel_id=1, source_target_pairs={{1,0},{2,1},{3,2},{5,4},{6,5},{7,6},{9,8},{10,9},{11,10},{13,12},{... | collective-permute-start | bytes 15368 | tf_op jit(solution)/shard_map/ppermute | solution.py:23
  442.9 7.4 %collective-permute-start.3 = (f32[2,5,1,128]{3,0,2,1:T(2,128)S(1)}, f32[2,5,1,128]{3,0,2,1:T(2,128)S(1)}, u32[]{:S(2)}, u32[]{:S(2)}) collective-permute-start(f32[2,5,1,128]{3,0,2,1:T(2,128)S(1)} %copy.230), channel_id=1, source_target_pairs={{0,1},{1,2},{2,3},{4,5},{5,6},{6,7},{8,9},{9,10},{10,11},{12,13},{... | collective-permute-start | bytes 15368 | tf_op jit(solution)/shard_map/ppermute | solution.py:20
Sparse Core Ops, SparseCore 0:
  20.1 27.8 all-gather.4
where the time goes:
time: 551 us; the launch traced here: 546 us
  local copies, waits for them, and re-layouts  296 us (54%)
  matrix products  87.6 us (16%)
  blocking collectives  59.1 us (11%)
  starting transfers between devices  44 us (8%)
  waiting for transfers between devices  27.5 us (5%)
  other arithmetic  16.9 us (3%)
  between operations  14.4 us (3%)
    unnamed x49, local copies, waits for them, and re-layouts  153 us
    all_to_all x3, local copies, waits for them, and re-layouts, to_modes(): lax.all_to_all(values, 'mode', split_axis=3, concat_axis=2, tiled=True)  43.7 us
    all_gather x1, blocking collectives, on_device(): full_map = lax.all_gather(mode_map, 'mode', axis=0, tiled=True)  40 us
    div x2, local copies, waits for them, and re-layouts, coupling_term(): return jnp.stack([real_part, imag_part]) / (NF * NK)  35.7 us
    all_gather x2, blocking collectives, entering(): pieces = lax.all_gather(value, axis)  19.1 us
    dot_general x5, matrix products, span_dft(): jnp.einsum('...k,kz->...z', imag_part, sine_part, precision=HIGHEST)  15.8 us
    all_to_all x2, waiting for transfers between devices, to_modes(): lax.all_to_all(values, 'mode', split_axis=3, concat_axis=2, tiled=True)  15.6 us
    dot_general x5, matrix products, span_dft(): real_cos = jnp.einsum('...k,kz->...z', real_part, cosine, precision=HIGHEST)  13.8 us
  transfers between devices with their start and end apart: 10, of which 5 were waited for; matrix products, arithmetic and copies ran while one was open for 9% of the time, Pallas kernels for 0%

commit v1 on v0

--- a/solution.py
+++ b/solution.py
@@ -138,7 +138,10 @@
 
 
 def to_modes(values):
-    return lax.all_to_all(values, "mode", split_axis=3, concat_axis=2, tiled=True)
+    return jnp.concatenate(
+        lax.all_to_all(jnp.stack(jnp.split(values, lax.axis_size("mode"), axis=3)), "mode", 0, 0),
+        axis=2,
+    )
 
 
 def on_device(adjoint, forward, mode_map):

time: 551 us -> 353 us (0.64)
  local copies, waits for them, and re-layouts: 296 us -> 109 us
  other arithmetic: 16.9 us -> 8.31 us
    unnamed x49 -> x105, local copies, waits for them, and re-layouts: 153 us -> 45.3 us
    all_to_all x3 -> x0, local copies, waits for them, and re-layouts: 43.7 us -> none  [to_modes(): lax.all_to_all(values, 'mode', split_axis=3, concat_axis=2, tiled=True)]
    div x2 -> x0, local copies, waits for them, and re-layouts: 35.7 us -> none  [coupling_term(): return jnp.stack([real_part, imag_part]) / (NF * NK)]
    all_to_all x2 -> x0, other arithmetic: 8.78 us -> none  [to_modes(): lax.all_to_all(values, 'mode', split_axis=3, concat_axis=2, tiled=True)]
  transfers between devices with their start and end apart: 10 -> 10, of which waited for: 5 -> 4; matrix products, arithmetic and copies ran while one was open for 9% -> 14% of each run, Pallas kernels for 0% -> 0%
where the time goes in v1:
time: 353 us; the launch traced here: 348 us
  local copies, waits for them, and re-layouts  109 us (31%)
  matrix products  86.2 us (24%)
  blocking collectives  59.1 us (17%)
  starting transfers between devices  44.5 us (13%)
  waiting for transfers between devices  26.7 us (8%)
  between operations  14.7 us (4%)
  other arithmetic  8.31 us (2%)
    unnamed x105, local copies, waits for them, and re-layouts  45.3 us
    all_gather x1, blocking collectives, on_device(): full_map = lax.all_gather(mode_map, 'mode', axis=0, tiled=True)  40 us
    all_gather x2, blocking collectives, entering(): pieces = lax.all_gather(value, axis)  19.1 us
    dot_general x5, matrix products, span_dft(): jnp.einsum('...k,kz->...z', imag_part, sine_part, precision=HIGHEST)  15.9 us
    all_to_all x2, waiting for transfers between devices, to_modes(): lax.all_to_all(jnp.stack(jnp.split(values, lax.axis_size('mode'), axis=3)...  15.4 us
    dot_general x5, matrix products, span_dft(): real_cos = jnp.einsum('...k,kz->...z', real_part, cosine, precision=HIGHEST)  13.8 us
    mul x10, local copies, waits for them, and re-layouts, coupling_term(): prod_real = w_real * a_real + w_imag * a_imag  13.2 us
    ppermute x2, starting transfers between devices, with_halo(): lax.ppermute(lax.slice_in_dim(block, block.shape[dim] - width, None, axis...  12.5 us
  transfers between devices with their start and end apart: 10, of which 4 were waited for; matrix products, arithmetic and copies ran while one was open for 14% of the time, Pallas kernels for 0%

profile of v1, /device:TPU:0, one launch (start us, length us, event | category | flops | bytes accessed | tf_op | source)
XLA Modules:
  0.0 348.2 jit_solution(16399125016380730434)
XLA Ops:
  6.5 3.5 copy.177
  10.0 7.6 %all-to-all-start.1 = ((f32[2,5,256,128]{3,1,0,2:T(8,128)}), f32[2,5,256,128]{3,1,0,2:T(8,128)S(1)}, u32[]{:S(2)}, u32[]{:S(2)}) async-start(f32[2,5,256,128]{3,1,0,2:T(8,128)} %copy.177), calls=%async_computation.1 | async-start | bytes 4194304 | tf_op jit(solution)/shard_map/all_to_all | solution.py:157
  18.3 40.0 %all-gather.2 = s32[32,1,128]{2,1,0:T(1,128)S(1)} all-gather(s32[1,1,128]{2,1,0:T(1,128)S(1)} %bitcast.535), channel_id=1, replica_groups=mesh['mode'=32,'wall'=2,'ckpt'=2] {'mode'}, dimensions={0}, use_global_device_ids=true | all-gather | bytes 16896 | tf_op jit(solution)/shard_map/all_gather | solution.py:153
  62.0 6.0 %all-to-all-start = ((f32[2,2,256,128]{3,1,0,2:T(2,128)}), f32[2,2,256,128]{3,1,0,2:T(2,128)}, u32[]{:S(2)}, u32[]{:S(2)}) async-start(f32[2,2,256,128]{3,1,0,2:T(2,128)} %copy.173), calls=%async_computation | async-start | bytes 1048576 | tf_op jit(solution)/shard_map/all_to_all | solution.py:158
  69.2 5.1 %fusion.66 = f32[64,5,8,64]{3,0,2,1:T(8,128)} fusion(f32[5,8,64,64]{3,2,1,0:T(8,128)S(1)} %reshape_squeeze.20), kind=kOutput, calls=%fused_computation.266 | convolution fusion | flops 125886464 | bytes 1310720 | tf_op jit(solution)/shard_map/...k,kz->...z/dot_general | solution.py:65
  74.3 5.1 %fusion.78 = f32[64,5,8,64]{3,0,2,1:T(8,128)} fusion(f32[5,8,64,64]{3,2,1,0:T(8,128)S(1)} %reshape_squeeze.20), kind=kOutput, calls=%fused_computation.278 | convolution fusion | flops 125886464 | bytes 1310720 | tf_op jit(solution)/shard_map/...k,kz->...z/dot_general | solution.py:66
  80.7 4.0 %convolution_subtract_fusion.7 = f32[64,5,8,64]{3,0,2,1:T(8,128)S(1)} fusion(f32[64,5,8,64]{3,0,2,1:T(8,128)S(1)} %copy-done.6, f32[5,8,64,64]{3,2,1,0:T(8,128)S(1)} %reshape_squeeze.21), kind=kOutput, calls=%fused_computation.17 | convolution fusion | flops 126050304 | bytes 1966080 | tf_op jit(solution)/shard_map/...k,kz->...z/dot_general | solution.py:68
  84.7 4.0 %convolution_add_fusion.7 = f32[64,5,8,64]{3,0,2,1:T(8,128)S(1)} fusion(f32[64,5,8,64]{3,0,2,1:T(8,128)S(1)} %copy-done.5, f32[5,8,64,64]{3,2,1,0:T(8,128)S(1)} %reshape_squeeze.21), kind=kOutput, calls=%fused_computation.16 | convolution fusion | flops 126050304 | bytes 1966080 | tf_op jit(solution)/shard_map/...k,kz->...z/dot_general | solution.py:67
  88.8 1.8 fusion.146
  92.3 2.5 convolution_add_fusion.3
  98.5 1.7 fusion.26
  112.9 3.2 multiply_subtract_fusion.1
  116.2 2.2 fusion.101
  120.4 2.4 fusion.21
  127.3 3.7 %convolution_subtract_fusion.6 = f32[5,8,64,64]{3,2,1,0:T(8,128)} fusion(f32[5,8,64,64]{3,2,1,0:T(8,128)} %fusion.21, f32[64,5,8,64]{3,2,1,0:T(8,128)S(1)} %reshape.115), kind=kOutput, calls=%fused_computation.15 | convolution fusion | flops 126054400 | bytes 1966080 | tf_op jit(solution)/shard_map/...k,kz->...z/dot_general | solution.py:68
  132.7 2.4 convolution_add_fusion.6
  156.9 7.5 %all-to-all-start.2 = ((f32[32,2,5,8,128]{4,3,2,1,0:T(8,128)}), f32[32,2,5,8,128]{4,3,2,1,0:T(8,128)}, u32[]{:S(2)}, u32[]{:S(2)}) async-start(f32[32,2,5,8,128]{4,3,2,1,0:T(8,128)} %constant_dynamic-update-slice_fusion), calls=%async_computation.2 | async-start | bytes 2621440 | tf_op jit(solution)/shard_map/all_to_all | solution.py:142
  165.8 6.4 %collective-permute-start.1 = (f32[2,5,1,128]{3,0,2,1:T(2,128)S(1)}, f32[2,5,1,128]{3,0,2,1:T(2,128)S(1)}, u32[]{:S(2)}, u32[]{:S(2)}) collective-permute-start(f32[2,5,1,128]{3,0,2,1:T(2,128)S(1)} %copy.219), channel_id=1, source_target_pairs={{0,1},{1,2},{2,3},{4,5},{5,6},{6,7},{8,9},{9,10},{10,11},{12,13},{... | collective-permute-start | bytes 15368 | tf_op jit(solution)/shard_map/ppermute | solution.py:20
  174.9 9.3 %all-to-all-done.2 = f32[32,2,5,8,128]{4,3,2,1,0:T(8,128)} async-done(((f32[32,2,5,8,128]{4,3,2,1,0:T(8,128)}), f32[32,2,5,8,128]{4,3,2,1,0:T(8,128)}, u32[]{:S(2)}, u32[]{:S(2)}) %all-to-all-start.2) | async-done | bytes 1310752 | tf_op jit(solution)/shard_map/all_to_all | solution.py:142
  187.1 2.6 fusion.9
  190.4 11.3 %all-gather = f32[8,1,128]{2,1,0:T(1,128)S(1)} all-gather(f32[2,1,128]{2,1,0:T(1,128)S(1)} %copy.187), channel_id=2, replica_groups=mesh['mode'=32,'wall'=2,'ckpt'=2] {'wall','ckpt'}, dimensions={0}, use_global_device_ids=true | all-gather | bytes 5120 | tf_op jit(solution)/shard_map/all_gather | solution.py:30
  202.8 2.1 copy.192
  204.9 4.1 %all-to-all-start.3 = ((f32[2,5,256,128]{3,0,1,2:T(2,128)}), f32[2,5,256,128]{3,0,1,2:T(2,128)S(1)}, u32[]{:S(2)}, u32[]{:S(2)}) async-start(f32[2,5,256,128]{3,0,1,2:T(2,128)} %copy.192), calls=%async_computation.3 | async-start | bytes 2621440 | tf_op jit(solution)/shard_map/all_to_all | solution.py:167
  209.0 2.1 mul.482
  211.1 2.5 mul.483
  213.6 2.1 mul.486
  215.7 2.5 mul.487
  218.2 10.4 %all-to-all-done.3 = f32[2,5,256,128]{3,0,1,2:T(2,128)S(1)} async-done(((f32[2,5,256,128]{3,0,1,2:T(2,128)}), f32[2,5,256,128]{3,0,1,2:T(2,128)S(1)}, u32[]{:S(2)}, u32[]{:S(2)}) %all-to-all-start.3) | async-done | bytes 1310752 | tf_op jit(solution)/shard_map/all_to_all | solution.py:167
  231.9 2.4 fusion.81
  234.4 2.4 fusion.71
  239.0 2.6 fusion
  241.6 1.8 copy.196
  243.5 2.5 reshape.116
  246.0 2.9 fusion.143
  251.8 1.8 copy.197
  257.8 1.8 fusion.100
  260.5 1.8 convolution_subtract_fusion
  263.6 2.5 fusion.15
  266.1 2.4 fusion.13
  271.6 3.8 %convolution_subtract_fusion.4 = f32[5,8,64,64]{3,2,1,0:T(8,128)} fusion(f32[5,8,64,64]{3,2,1,0:T(8,128)} %fusion.15, f32[64,5,8,64]{3,2,1,0:T(8,128)S(1)} %reshape.119), kind=kOutput, calls=%fused_computation.11 | convolution fusion | flops 126054400 | bytes 1966080 | tf_op jit(solution)/shard_map/...k,kz->...z/dot_general | solution.py:68
  275.4 2.6 stack_reshape.14
  277.9 3.7 %convolution_add_fusion.4 = f32[5,8,64,64]{3,2,1,0:T(8,128)} fusion(f32[5,8,64,64]{3,2,1,0:T(8,128)} %fusion.13, f32[64,5,8,64]{3,2,1,0:T(8,128)S(1)} %reshape.119), kind=kOutput, calls=%fused_computation.10 | convolution fusion | flops 126050304 | bytes 1966080 | tf_op jit(solution)/shard_map/...k,kz->...z/dot_general | solution.py:67
  281.7 1.8 stack_reshape.15
  303.5 4.2 %all-to-all-start.4 = ((f32[32,2,5,8,128]{4,3,2,1,0:T(8,128)}), f32[32,2,5,8,128]{4,3,2,1,0:T(8,128)S(1)}, u32[]{:S(2)}, u32[]{:S(2)}) async-start(f32[32,2,5,8,128]{4,3,2,1,0:T(8,128)} %constant_dynamic-update-slice_fusion.32), calls=%async_computation.4 | async-start | bytes 2621440 | tf_op jit(solution)/shard_map/all_to_all | solution.py:142
  313.0 6.1 %collective-permute-start.3 = (f32[2,5,1,128]{3,0,2,1:T(2,128)S(1)}, f32[2,5,1,128]{3,0,2,1:T(2,128)S(1)}, u32[]{:S(2)}, u32[]{:S(2)}) collective-permute-start(f32[2,5,1,128]{3,0,2,1:T(2,128)S(1)} %copy.190), channel_id=1, source_target_pairs={{0,1},{1,2},{2,3},{4,5},{5,6},{6,7},{8,9},{9,10},{10,11},{12,13},{... | collective-permute-start | bytes 15368 | tf_op jit(solution)/shard_map/ppermute | solution.py:20
  321.5 6.1 %all-to-all-done.4 = f32[32,2,5,8,128]{4,3,2,1,0:T(8,128)S(1)} async-done(((f32[32,2,5,8,128]{4,3,2,1,0:T(8,128)}), f32[32,2,5,8,128]{4,3,2,1,0:T(8,128)S(1)}, u32[]{:S(2)}, u32[]{:S(2)}) %all-to-all-start.4) | async-done | bytes 1310752 | tf_op jit(solution)/shard_map/all_to_all | solution.py:142
  328.1 2.7 copy_subtract_fusion
  331.4 7.8 %all-gather.1 = f32[8,1,128]{2,1,0:T(1,128)S(1)} all-gather(f32[2,1,128]{2,1,0:T(1,128)S(1)} %copy.204), channel_id=3, replica_groups=mesh['mode'=32,'wall'=2,'ckpt'=2] {'wall','ckpt'}, dimensions={0}, use_global_device_ids=true | all-gather | bytes 5120 | tf_op jit(solution)/shard_map/all_gather | solution.py:30
  (219 shorter events, 111.9 us)
Async XLA Ops:
  10.0 8.3 %copy-start.18 = (s32[128]{0:T(128)S(1)}, s32[128]{0:T(128)}, u32[]{:S(2)}) copy-start(s32[128]{0:T(128)} %param.9) | copy-start | bytes 1540
  10.0 52.0 %all-to-all-start.1 = ((f32[2,5,256,128]{3,1,0,2:T(8,128)}), f32[2,5,256,128]{3,1,0,2:T(8,128)S(1)}, u32[]{:S(2)}, u32[]{:S(2)}) async-start(f32[2,5,256,128]{3,1,0,2:T(8,128)} %copy.177), calls=%async_computation.1 | async-start | bytes 4194304 | tf_op jit(solution)/shard_map/all_to_all | solution.py:157
  17.6 42.1 %all-gather.5.cloned.1.call-start = ((), (), s32[]{:S(2)}) async-start(), calls=%async_computation.5 | async-start | bytes 1572864 | tf_op jit(solution)/shard_map/all_gather | solution.py:150
  62.0 32.7 %all-to-all-start = ((f32[2,2,256,128]{3,1,0,2:T(2,128)}), f32[2,2,256,128]{3,1,0,2:T(2,128)}, u32[]{:S(2)}, u32[]{:S(2)}) async-start(f32[2,2,256,128]{3,1,0,2:T(2,128)} %copy.173), calls=%async_computation | async-start | bytes 1048576 | tf_op jit(solution)/shard_map/all_to_all | solution.py:158
  79.4 1.3 copy-start.6
  80.7 4.0 %copy-start.5 = (f32[64,5,8,64]{3,0,2,1:T(8,128)S(1)}, f32[64,5,8,64]{3,0,2,1:T(8,128)}, u32[]{:S(2)}) copy-start(f32[64,5,8,64]{3,0,2,1:T(8,128)} %fusion.78) | copy-start | bytes 1966084
  105.7 1.0 copy-start.17
  122.8 1.3 copy-start.12
  156.9 7.6 %copy-start.3 = (f32[2,5,256,128]{3,2,1,0:T(8,128)S(1)}, f32[2,5,256,128]{3,2,1,0:T(8,128)}, u32[]{:S(2)}) copy-start(f32[2,5,256,128]{3,2,1,0:T(8,128)} %param.7) | copy-start | bytes 3932164
  156.9 27.3 %all-to-all-start.2 = ((f32[32,2,5,8,128]{4,3,2,1,0:T(8,128)}), f32[32,2,5,8,128]{4,3,2,1,0:T(8,128)}, u32[]{:S(2)}, u32[]{:S(2)}) async-start(f32[32,2,5,8,128]{4,3,2,1,0:T(8,128)} %constant_dynamic-update-slice_fusion), calls=%async_computation.2 | async-start | bytes 2621440 | tf_op jit(solution)/shard_map/all_to_all | solution.py:142
  164.5 8.2 %collective-permute-start = (f32[2,5,1,128]{3,0,2,1:T(2,128)S(1)}, f32[2,5,1,128]{3,0,2,1:T(2,128)S(1)}, u32[]{:S(2)}, u32[]{:S(2)}) collective-permute-start(f32[2,5,1,128]{3,0,2,1:T(2,128)S(1)} %copy.218), channel_id=1, source_target_pairs={{1,0},{2,1},{3,2},{5,4},{6,5},{7,6},{9,8},{10,9},{11,10},{13,12},{... | collective-permute-start | bytes 15368 | tf_op jit(solution)/shard_map/ppermute | solution.py:23
  165.8 8.0 %collective-permute-start.1 = (f32[2,5,1,128]{3,0,2,1:T(2,128)S(1)}, f32[2,5,1,128]{3,0,2,1:T(2,128)S(1)}, u32[]{:S(2)}, u32[]{:S(2)}) collective-permute-start(f32[2,5,1,128]{3,0,2,1:T(2,128)S(1)} %copy.219), channel_id=1, source_target_pairs={{0,1},{1,2},{2,3},{4,5},{5,6},{6,7},{8,9},{9,10},{10,11},{12,13},{... | collective-permute-start | bytes 15368 | tf_op jit(solution)/shard_map/ppermute | solution.py:20
  189.9 12.1 %copy-start.15 = (f32[2,1,256,128]{2,3,0,1:T(8,128)}, f32[2,1,256,128]{2,3,0,1:T(8,128)S(1)}, u32[]{:S(2)}) copy-start(f32[2,1,256,128]{2,3,0,1:T(8,128)S(1)} %slice.157) | copy-start | bytes 786436
  202.0 0.7 copy-start.16
  204.9 23.7 %all-to-all-start.3 = ((f32[2,5,256,128]{3,0,1,2:T(2,128)}), f32[2,5,256,128]{3,0,1,2:T(2,128)S(1)}, u32[]{:S(2)}, u32[]{:S(2)}) async-start(f32[2,5,256,128]{3,0,1,2:T(2,128)} %copy.192), calls=%async_computation.3 | async-start | bytes 2621440 | tf_op jit(solution)/shard_map/all_to_all | solution.py:167
  234.4 2.4 copy-start.8
  246.0 2.9 copy-start.2
  246.0 4.6 %copy-start.4 = (f32[5,8,64,64]{3,2,1,0:T(8,128)S(1)}, f32[5,8,64,64]{3,2,1,0:T(8,128)}, u32[]{:S(2)}) copy-start(f32[5,8,64,64]{3,2,1,0:T(8,128)} %fusion.81) | copy-start | bytes 1966084
  253.6 1.7 copy-start.13
  255.4 1.1 copy-start.7
  255.4 1.3 copy-start.9
  255.4 1.5 copy-start.10
  257.8 2.7 copy-start
  266.1 2.4 copy-start.1
  266.1 2.4 copy-start.11
  281.7 1.8 copy-start.14
  303.5 24.0 %all-to-all-start.4 = ((f32[32,2,5,8,128]{4,3,2,1,0:T(8,128)}), f32[32,2,5,8,128]{4,3,2,1,0:T(8,128)S(1)}, u32[]{:S(2)}, u32[]{:S(2)}) async-start(f32[32,2,5,8,128]{4,3,2,1,0:T(8,128)} %constant_dynamic-update-slice_fusion.32), calls=%async_computation.4 | async-start | bytes 2621440 | tf_op jit(solution)/shard_map/all_to_all | solution.py:142
  310.4 8.7 %collective-permute-start.2 = (f32[2,5,1,128]{3,0,2,1:T(2,128)S(1)}, f32[2,5,1,128]{3,0,2,1:T(2,128)S(1)}, u32[]{:S(2)}, u32[]{:S(2)}) collective-permute-start(f32[2,5,1,128]{3,0,2,1:T(2,128)S(1)} %copy.188), channel_id=1, source_target_pairs={{1,0},{2,1},{3,2},{5,4},{6,5},{7,6},{9,8},{10,9},{11,10},{13,12},{... | collective-permute-start | bytes 15368 | tf_op jit(solution)/shard_map/ppermute | solution.py:23
  313.0 7.4 %collective-permute-start.3 = (f32[2,5,1,128]{3,0,2,1:T(2,128)S(1)}, f32[2,5,1,128]{3,0,2,1:T(2,128)S(1)}, u32[]{:S(2)}, u32[]{:S(2)}) collective-permute-start(f32[2,5,1,128]{3,0,2,1:T(2,128)S(1)} %copy.190), channel_id=1, source_target_pairs={{0,1},{1,2},{2,3},{4,5},{5,6},{6,7},{8,9},{9,10},{10,11},{12,13},{... | collective-permute-start | bytes 15368 | tf_op jit(solution)/shard_map/ppermute | solution.py:20
Sparse Core Ops, SparseCore 0:
  20.0 27.8 all-gather.4
